TPU v7x, 32 devices: a whole 2x2x4 slice. The times are simulated.
32 devices in a mesh: groups: 2 (over y), filt: 4 (over z), sp: 2 (over x), in: 2 (over core).
Axes of the slice: x: 2, y: 2, z: 4, core: 2. Of those that a mesh axis runs over, the one named last changes fastest.
Arguments:
- image: bfloat16 [16, 256, 1024], P(('groups', 'sp', 'filt'), None, 'in'), parts along dimension 0, may hold values from -6 to 6
- weight: bfloat16 [3, 3, 1024, 1024], P(None, None, 'filt'), may hold values from -0.0625 to 0.0625
- bias: float32 [1024], P('filt'), may hold values from -3 to 3
- cotangent: bfloat16 [16, 1024, 256], P(('groups', 'sp'), 'filt'), parts along dimension 0, may hold values from -0.029907227 to 0.029907227
Outputs:
- output: bfloat16 [16, 1024, 256], P(('groups', 'sp', 'filt'), None, 'in'), parts along dimension 0
- grad_weight: float32 [6, 3, 1024, 1024], P('groups', None, 'filt', 'in'), parts along dimension 0
- grad_bias: float32 [2048], P(('groups', 'filt')), parts along dimension 0
There are 2 independent parts, one for each index of `groups`. A program takes and returns all parts, laid end to end along the dimension named above; an argument that names none is the same for every part. Nothing has to cross between parts.
All inputs are finite; a program needn't handle non-finite values.
Results may differ from a plain program's by a relative error of at most 0.0055.
Values may be sent and summed in bfloat16 or wider, within the bound.
A program may use at most 64 MiB of HBM per device.

v0:
```python
import jax
import jax.numpy as jnp
from jax import lax
from jax.sharding import PartitionSpec as P


def with_halo(array, sides, width):
    for axis, dim in sides:
        size, length = (lax.axis_size(axis), array.shape[dim])
        up = [(i, (i + 1) % size) for i in range(size - 1)]
        down = [(j, i) for i, j in up]
        last = lax.slice_in_dim(array, length - width, length, axis=dim)
        initial = lax.slice_in_dim(array, 0, width, axis=dim)
        before = lax.ppermute(last, axis, up)
        after = lax.ppermute(initial, axis, down)
        array = jnp.concatenate([before, array, after], axis=dim)
    return array


def tap_products(padded, weight, row_count, col_count):
    running = jnp.zeros((row_count, weight.shape[2], col_count), jnp.float32)
    for row_tap in range(3):
        for col_tap in range(3):
            window = padded[row_tap : row_tap + row_count, col_tap : col_tap + col_count]
            running = running + jnp.einsum(
                "rwc,dc->rdw", window, weight[row_tap, col_tap], preferred_element_type=jnp.float32
            )
    return running


def tap_gradients(padded, grad_out, row_count, col_count):
    pieces = []
    for row_tap in range(3):
        for col_tap in range(3):
            window = padded[row_tap : row_tap + row_count, col_tap : col_tap + col_count]
            pieces.append(
                jnp.einsum("rwc,rdw->dc", window, grad_out, preferred_element_type=jnp.float32)
            )
    stacked = jnp.stack(pieces)
    return stacked.reshape(3, 3, stacked.shape[1], stacked.shape[2])


def silu_parts(shifted, cotangent):
    sigmoid_v = jax.nn.sigmoid(shifted)
    slope = sigmoid_v * (1.0 + shifted * (1.0 - sigmoid_v))
    grad_out = (cotangent.astype(jnp.float32) * slope).astype(jnp.bfloat16)
    return (sigmoid_v, grad_out)


def on_device(image, weight, bias, cotangent):
    row_count = cotangent.shape[0]
    full_cols = cotangent.shape[2]
    in_count = lax.axis_size("in")
    half_cols = full_cols // in_count
    channels = weight.shape[3]
    own_channels = channels // in_count
    bias_col = bias[None, :, None]
    panel = lax.all_gather(image, "filt", axis=0, tiled=True)
    bordered = with_halo(panel, (("sp", 0),), 1)
    padded = jnp.pad(bordered, ((0, 0), (1, 1), (0, 0)))
    own_weight = lax.dynamic_slice_in_dim(
        weight, lax.axis_index("in") * own_channels, own_channels, 3
    )
    partial_value = tap_products(padded, own_weight, row_count, full_cols)
    shifted = lax.psum(partial_value, "in") + bias_col
    sigmoid_v, grad_out = silu_parts(shifted, cotangent)
    local_weight = tap_gradients(padded, grad_out, row_count, full_cols)
    local_bias = jnp.sum(grad_out.astype(jnp.float32), axis=(0, 2))
    grad_weight, grad_bias = lax.psum((local_weight, local_bias), "sp")
    first_col = lax.axis_index("in") * half_cols
    own_shift = lax.dynamic_slice_in_dim(shifted, first_col, half_cols, 2)
    own_sigmoid = lax.dynamic_slice_in_dim(sigmoid_v, first_col, half_cols, 2)
    activated = own_shift * own_sigmoid
    output = lax.all_to_all(
        activated.astype(jnp.bfloat16), "filt", split_axis=0, concat_axis=1, tiled=True
    )
    return (output, grad_weight, grad_bias)


def solution(mesh):
    placed = (
        P(("groups", "sp", "filt"), None, "in"),
        P(None, None, "filt", None),
        P("filt"),
        P(("groups", "sp"), "filt", None),
    )
    return jax.shard_map(
        on_device,
        mesh=mesh,
        in_specs=placed,
        out_specs=(
            P(("groups", "sp", "filt"), None, "in"),
            P("groups", None, "filt", "in"),
            P(("groups", "filt")),
        ),
        check_vma=False,
    )
```

profile of v0, /device:TPU:0, one launch (start us, length us, event | category | flops | bytes accessed | tf_op | source)
XLA Modules:
  0.0 229.2 jit_solution(2796276300759234209)
XLA Ops:
  7.9 32.3 %all-gather.2.cloned.1.call-done = bf16[4,256,512]{2,1,0:T(8,128)(2,1)} async-done(((bf16[1,256,512]{2,1,0:T(8,128)(2,1)}), bf16[4,256,512]{2,1,0:T(8,128)(2,1)}) %all-gather.2.cloned.1.call-update) | async-done | bytes 1048592 | tf_op jit(solution)/shard_map/all_gather | solution.py:58
  40.3 1.1 fusion.54
  41.3 3.4 %collective-permute-start = (bf16[1,256,512]{2,1,0:T(8,128)(2,1)S(1)}, bf16[1,256,512]{2,1,0:T(8,128)(2,1)S(1)}, u32[]{:S(2)}, u32[]{:S(2)}) collective-permute-start(bf16[1,256,512]{2,1,0:T(8,128)(2,1)S(1)} %get-tuple-element.6), channel_id=1, source_target_pairs={{0,2},{1,3},{4,6},{5,7},{8,10},{9,11},{12,14},{13,15},{16,18},{17,... | collective-permute-start | bytes 786440 | tf_op jit(solution)/shard_map/ppermute | solution.py:14
  44.7 1.3 collective-permute-start.1
  46.0 1.8 fusion.40
  47.8 2.0 collective-permute-done
  49.8 4.1 %collective-permute-done.1 = bf16[1,256,512]{2,1,0:T(8,128)(2,1)S(1)} collective-permute-done((bf16[1,256,512]{2,1,0:T(8,128)(2,1)S(1)}, bf16[1,256,512]{2,1,0:T(8,128)(2,1)S(1)}, u32[]{:S(2)}, u32[]{:S(2)}) %collective-permute-start.1) | collective-permute-done | bytes 262176 | tf_op jit(solution)/shard_map/ppermute | solution.py:15
  53.9 1.6 fusion.5
  55.6 1.5 fusion.31
  57.1 1.4 fusion.26
  58.5 1.4 fusion.34
  59.9 1.4 fusion.23
  61.4 1.4 fusion.38
  62.8 1.5 fusion.12
  64.3 1.4 fusion.39
  65.7 2.5 %fusion.9 = f32[4,256,256]{2,1,0:T(8,128)} fusion(f32[256,4,256]{2,0,1:T(8,128)S(1)} %fusion.23, f32[256,4,256]{2,0,1:T(8,128)S(1)} %fusion.39, f32[256,4,256]{2,0,1:T(8,128)S(1)} %fusion.26, f32[256,4,256]{2,0,1:T(8,128)S(1)} %fusion.12, bf16[6,258,512]{2,1,0:T(8,128)(2,1)S(1)} %fusion.5, bf16[3,3,256,1024]{3,2,1,0:T(8,128)(2,1)} %param.5, s32[]{:T(128)S(6)} %add.78, ...), kind=kOutput, calls=%fused_computation.12 | convolution fusion | flops 269484032 | bytes 6553612 | tf_op jit(solution)/shard_map/rwc,dc->rdw/dot_general | solution.py:25
  68.3 18.6 %all-reduce.4.cloned.1.call-done = f32[4,256,256]{2,1,0:T(8,128)} async-done(((f32[4,256,256]{2,1,0:T(8,128)}), f32[4,256,256]{2,1,0:T(8,128)}) %all-reduce.4.cloned.1.call-update) | async-done | bytes 1048592 | tf_op jit(solution)/shard_map/psum | solution.py:65
  86.9 3.0 %convert_reduce_fusion = (f32[256]{0:T(256)S(1)}, bf16[4,256,256]{2,1,0:T(8,128)(2,1)S(1)}, f32[4,256,256]{2,1,0:T(8,128)}) fusion(bf16[4,256,256]{2,1,0:T(8,128)(2,1)} %param.7, f32[4,256,256]{2,1,0:T(8,128)} %all-reduce.4.cloned.1.call-done, f32[256]{0:T(256)S(1)} %copy-done.3), kind=kLoop, calls=%fused_computation.37 | loop fusion | flops 3407616 | bytes 3147776 | tf_op jit(solution)/shard_map/reduce_sum | solution.py:68
  94.0 2.2 copy-done.2
  97.3 4.9 %all-to-all-start = ((bf16[4,256,128]{2,1,0:T(8,128)(2,1)}), bf16[4,256,128]{2,1,0:T(8,128)(2,1)S(1)}, u32[]{:S(2)}, u32[]{:S(2)}) async-start(bf16[4,256,128]{2,1,0:T(8,128)(2,1)} %multiply_convert_fusion.1), calls=%async_computation | async-start | bytes 524288 | tf_op jit(solution)/shard_map/all_to_all | solution.py:74
  102.2 5.7 %psum.23 = f32[256]{0:T(256)} all-reduce(f32[256]{0:T(256)S(1)} %get-tuple-element.3), channel_id=1, replica_groups=mesh['groups'=2,'filt'=4,'sp'=2,'in'=2] {'sp'}, use_global_device_ids=true, to_apply=%region_3.4 | all-reduce | flops 256 | bytes 2048 | tf_op jit(solution)/shard_map/psum | solution.py:69
  107.8 3.6 %all-to-all-done = bf16[4,256,128]{2,1,0:T(8,128)(2,1)S(1)} async-done(((bf16[4,256,128]{2,1,0:T(8,128)(2,1)}), bf16[4,256,128]{2,1,0:T(8,128)(2,1)S(1)}, u32[]{:S(2)}, u32[]{:S(2)}) %all-to-all-start) | async-done | bytes 262176 | tf_op jit(solution)/shard_map/all_to_all | solution.py:74
  111.5 105.4 %all-reduce.6.cloned.1.call-done = f32[3,3,256,512]{3,2,1,0:T(8,128)} async-done(((f32[3,3,256,512]{3,2,1,0:T(8,128)}), f32[3,3,256,512]{3,2,1,0:T(8,128)}) %all-reduce.6.cloned.1.call-update) | async-done | bytes 4718608 | tf_op jit(solution)/shard_map/psum | solution.py:69
  217.6 5.0 %copy.19 = f32[3,3,256,512]{3,2,1,0:T(8,128)} copy(f32[3,3,256,512]{3,2,1,0:T(8,128)} %all-reduce.6.cloned.1.call-done) | data formatting | bytes 9437184
  (25 shorter events, 6.7 us)
Async XLA Ops:
  7.2 33.1 %all-gather.2.cloned.1.call-start = ((), (), s32[]{:S(2)}) async-start(), calls=%async_computation.1 | async-start | bytes 1310720 | tf_op jit(solution)/shard_map/all_gather | solution.py:58
  7.9 79.0 %all-reduce.4.cloned.1.call-start = ((), (), s32[]{:S(2)}) async-start(), calls=%async_computation.2 | async-start | bytes 2097152 | tf_op jit(solution)/shard_map/psum | solution.py:65
  41.3 8.4 %collective-permute-start = (bf16[1,256,512]{2,1,0:T(8,128)(2,1)S(1)}, bf16[1,256,512]{2,1,0:T(8,128)(2,1)S(1)}, u32[]{:S(2)}, u32[]{:S(2)}) collective-permute-start(bf16[1,256,512]{2,1,0:T(8,128)(2,1)S(1)} %get-tuple-element.6), channel_id=1, source_target_pairs={{0,2},{1,3},{4,6},{5,7},{8,10},{9,11},{12,14},{13,15},{16,18},{17,... | collective-permute-start | bytes 786440 | tf_op jit(solution)/shard_map/ppermute | solution.py:14
  44.7 9.2 %collective-permute-start.1 = (bf16[1,256,512]{2,1,0:T(8,128)(2,1)S(1)}, bf16[1,256,512]{2,1,0:T(8,128)(2,1)S(1)}, u32[]{:S(2)}, u32[]{:S(2)}) collective-permute-start(bf16[1,256,512]{2,1,0:T(8,128)(2,1)S(1)} %get-tuple-element.7), channel_id=1, source_target_pairs={{2,0},{3,1},{6,4},{7,5},{10,8},{11,9},{14,12},{15,13},{18,16},{19,... | collective-permute-start | bytes 786440 | tf_op jit(solution)/shard_map/ppermute | solution.py:15
  55.5 5.9 %copy-start = (bf16[4,256,512]{2,1,0:T(8,128)(2,1)S(1)}, bf16[4,256,512]{2,1,0:T(8,128)(2,1)}, u32[]{:S(2)}) copy-start(bf16[4,256,512]{2,1,0:T(8,128)(2,1)} %all-gather.2.cloned.1.call-done) | copy-start | bytes 3145732
  64.3 22.6 %copy-start.3 = (f32[256]{0:T(256)S(1)}, f32[256]{0:T(256)}, u32[]{:S(2)}) copy-start(f32[256]{0:T(256)} %param.6) | copy-start | bytes 3076
  68.3 148.6 %all-reduce.6.cloned.1.call-start = ((), (), s32[]{:S(2)}) async-start(), calls=%async_computation.3 | async-start | bytes 9437184 | tf_op jit(solution)/shard_map/psum | solution.py:69
  93.5 2.7 %copy-start.1 = (f32[4,256,256]{2,1,0:T(8,128)S(1)}, f32[4,256,256]{2,1,0:T(8,128)}, u32[]{:S(2)}) copy-start(f32[4,256,256]{2,1,0:T(8,128)} %get-tuple-element.5) | copy-start | bytes 3145732
  94.0 2.2 copy-start.2
  97.3 14.2 %all-to-all-start = ((bf16[4,256,128]{2,1,0:T(8,128)(2,1)}), bf16[4,256,128]{2,1,0:T(8,128)(2,1)S(1)}, u32[]{:S(2)}, u32[]{:S(2)}) async-start(bf16[4,256,128]{2,1,0:T(8,128)(2,1)} %multiply_convert_fusion.1), calls=%async_computation | async-start | bytes 524288 | tf_op jit(solution)/shard_map/all_to_all | solution.py:74
Sparse Core Ops, SparseCore 0:
  9.5 30.6 all-gather.1
  68.4 18.4 all-reduce.3
  96.3 120.5 all-reduce.5
where the time goes:
time: 230 us; the launch traced here: 229 us
  waiting for transfers between devices  167 us (73%)
  matrix products  18.4 us (8%)
  between operations  14 us (6%)
  starting transfers between devices  9.68 us (4%)
  local copies, waits for them, and re-layouts  8.99 us (4%)
  blocking collectives  5.67 us (2%)
  other arithmetic  5.65 us (2%)
    psum x1, waiting for transfers between devices, on_device(): grad_weight, grad_bias = lax.psum((local_weight, local_bias), 'sp')  105 us
    all_gather x1, waiting for transfers between devices, on_device(): panel = lax.all_gather(image, 'filt', axis=0, tiled=True)  32.3 us
    psum x1, waiting for transfers between devices, on_device(): shifted = lax.psum(partial_value, 'in') + bias_col  18.6 us
    dot_general x9, matrix products, tap_products(): jnp.einsum('rwc,dc->rdw', window, weight[row_tap, col_tap], preferred_ele...  14.4 us
    unnamed x10, local copies, waits for them, and re-layouts  7.93 us
    psum x1, blocking collectives, on_device(): grad_weight, grad_bias = lax.psum((local_weight, local_bias), 'sp')  5.67 us
    all_to_all x1, starting transfers between devices, on_device(): lax.all_to_all(activated.astype(jnp.bfloat16), 'filt', split_axis=0, conc...  4.88 us
  transfers between devices with their start and end apart: 6, of which 6 were waited for; matrix products, arithmetic and copies ran while one was open for 1% of the time, Pallas kernels for 0%

commit v1 on v0

v1 whole, which is shorter than its diff:
```python
import functools

import jax
import jax.numpy as jnp
from jax import lax
from jax.experimental import pallas as pl
from jax.experimental.pallas import tpu as pltpu
from jax.sharding import PartitionSpec as P

MESH = pl.DeviceIdType.MESH
NT = (((1,), (1,)), ((), ()))


def shift_cols(value, by):
    cols = value.shape[1]
    col = lax.broadcasted_iota(jnp.int32, value.shape, 1)
    if by < 0:
        return jnp.where(col == 0, 0.0, pltpu.roll(value, 1, 1))
    return jnp.where(col == cols - 1, 0.0, pltpu.roll(value, cols - 1, 1))


def kernel(
    n_f, n_s,
    image, weight, bias, cotangent,
    out, gw, gb,
    rows, w, cot, part, peer, grads, act, gw_acc,
    load_sem, row_send, row_recv, x_send, sum_send, sum_recv,
    g_send, g_recv, h_send, h_recv, out_send, out_recv, gw_sem,
):
    p, s, c = lax.axis_index("filt"), lax.axis_index("sp"), lax.axis_index("in")
    sibling = 1 - c
    cols, depth = rows.shape[1], rows.shape[2]
    o = w.shape[2]
    half_o, half_c = o // 2, cols // 2
    total = n_f * n_s
    first = s * n_f
    x_peers = [lax.rem(s + d, n_s) for d in range(1, n_s)]

    load_row = pltpu.make_async_copy(image.at[0], rows.at[1 + first + p], load_sem.at[0])
    load_w = pltpu.make_async_copy(
        weight.at[:, :, :, pl.ds(pl.multiple_of(c * depth, depth), depth)], w, load_sem.at[1]
    )
    load_cot = pltpu.make_async_copy(cotangent, cot, load_sem.at[2])
    load_row.start()
    load_w.start()
    load_cot.start()

    barrier = pltpu.get_barrier_semaphore()
    for d in range(1, n_f):
        pl.semaphore_signal(barrier, 1, device_id={"filt": lax.rem(p + d, n_f)}, device_id_type=MESH)
    for peer_s in x_peers:
        pl.semaphore_signal(barrier, 1, device_id={"sp": peer_s}, device_id_type=MESH)
    pl.semaphore_signal(barrier, 1, device_id={"in": sibling}, device_id_type=MESH)
    zero = jnp.zeros((cols, depth), rows.dtype)
    rows[0] = zero
    rows[total + 1] = zero
    pl.semaphore_wait(barrier, n_f - 1 + n_s - 1 + 1)

    def row_copy(q, way, where, send):
        slot = rows.at[1 + q]
        return pltpu.make_async_remote_copy(
            src_ref=slot, dst_ref=slot, send_sem=send, recv_sem=row_recv.at[q],
            device_id={way: where}, device_id_type=MESH,
        )

    def to_right(q):
        return row_copy(first + q, "filt", p + 1, row_send.at[0, q])

    def to_left(q):
        return row_copy(first + q, "filt", p - 1, row_send.at[1, q])

    def to_x(q, d):
        return row_copy(first + q, "sp", x_peers[d], x_send.at[d, q])

    def wait_row(q):
        row_copy(q, "filt", p, row_send.at[0, 0]).wait_recv()

    def pass_on(q, right, left):
        if right:
            @pl.when(p + 1 < n_f)
            def _():
                to_right(q).start()
        if left:
            @pl.when(p >= 1)
            def _():
                to_left(q).start()
        for d in range(n_s - 1):
            to_x(q, d).start()

    load_row.wait()
    pass_on(p, True, True)
    for t in range(1, n_f):
        @pl.when(p - t >= 0)
        def _():
            wait_row(first + p - t)
            pass_on(p - t, True, False)

        @pl.when(p + t < n_f)
        def _():
            wait_row(first + p + t)
            pass_on(p + t, False, True)

    load_w.wait()
    load_cot.wait()

    @pl.when(s > 0)
    def _():
        wait_row(first - 1)

    @pl.when(s + 1 < n_s)
    def _():
        wait_row(first + n_f)

    def sum_copy(r):
        return pltpu.make_async_remote_copy(
            src_ref=part.at[r], dst_ref=peer.at[r], send_sem=sum_send.at[r], recv_sem=sum_recv.at[r],
            device_id={"in": sibling}, device_id_type=MESH,
        )

    @pl.loop(0, n_f)
    def _(r):
        sums = jnp.zeros((3 * o, cols), jnp.float32)
        for a in range(3):
            sums = sums + lax.dot_general(
                w[a].reshape(3 * o, depth), rows[first + r + a], NT, preferred_element_type=jnp.float32
            )
        part[r] = shift_cols(sums[:o], -1) + sums[o:2 * o] + shift_cols(sums[2 * o:], 1)
        sum_copy(r).start()

    bias_all = jnp.broadcast_to(bias[...], (cols, o)).T

    def out_copy(r):
        return pltpu.make_async_remote_copy(
            src_ref=act.at[r, :, pl.ds(pl.multiple_of(c * half_c, half_c), half_c)],
            dst_ref=out.at[0, pl.ds(pl.multiple_of(p * o, o), o), :],
            send_sem=out_send.at[r], recv_sem=out_recv.at[p],
            device_id={"filt": r}, device_id_type=MESH,
        )

    own_out = pltpu.make_async_copy(
        act.at[p, :, pl.ds(pl.multiple_of(c * half_c, half_c), half_c)],
        out.at[0, pl.ds(pl.multiple_of(p * o, o), o), :],
        load_sem.at[0],
    )

    def lanes(q, count=1):
        return pl.ds(pl.multiple_of(q * cols, cols), count * cols)

    @pl.loop(0, n_f)
    def _(r):
        sum_copy(r).wait_recv()
        shifted = part[r] + peer[r] + bias_all
        sig = jax.nn.sigmoid(shifted)
        act[r] = (shifted * sig).astype(jnp.bfloat16)
        slope = sig * (1.0 + shifted * (1.0 - sig))
        grad = (cot[r].astype(jnp.float32) * slope).astype(jnp.bfloat16)
        grads[1, :, lanes(first + r)] = grad
        wide = grad.astype(jnp.float32)
        grads[0, :, lanes(first + r)] = shift_cols(wide, 1).astype(jnp.bfloat16)
        grads[2, :, lanes(first + r)] = shift_cols(wide, -1).astype(jnp.bfloat16)

        @pl.when(r == p)
        def _():
            own_out.start()

        @pl.when(r != p)
        def _():
            out_copy(r).start()

    def g_part(block, core):
        return grads.at[
            1, pl.ds(pl.multiple_of(core * half_o, half_o), half_o), lanes(block * n_f, n_f)
        ]

    def g_copy(d):
        return pltpu.make_async_remote_copy(
            src_ref=g_part(s, c), dst_ref=g_part(s, c), send_sem=g_send.at[d], recv_sem=g_recv.at[s],
            device_id={"sp": x_peers[d]}, device_id_type=MESH,
        )

    def g_wait(block, core, recv):
        pltpu.make_async_remote_copy(
            src_ref=g_part(block, core), dst_ref=g_part(block, core), send_sem=g_send.at[0], recv_sem=recv,
            device_id={"in": sibling}, device_id_type=MESH,
        ).wait_recv()

    def h_copy(d):
        block = x_peers[d]
        return pltpu.make_async_remote_copy(
            src_ref=g_part(block, c), dst_ref=g_part(block, c), send_sem=h_send.at[d], recv_sem=h_recv.at[block],
            device_id={"in": sibling}, device_id_type=MESH,
        )

    for d in range(n_s - 1):
        g_copy(d).start()

    def tap(a, b, block):
        window = rows[pl.ds(block * n_f + a, n_f)].reshape(n_f * cols, depth)
        return jnp.dot(
            grads[b, :, lanes(block * n_f, n_f)], window, preferred_element_type=jnp.float32
        )

    @pl.loop(0, 9)
    def _(k):
        gw_acc[k] = tap(k // 3, lax.rem(k, 3), s)

    for d in range(n_s - 1):
        g_wait(x_peers[d], c, g_recv.at[x_peers[d]])
        h_copy(d).start()

    for d in range(n_s - 1):
        for q in range(n_f):
            row = x_peers[d] * n_f + q

            @pl.when((row != first - 1) & (row != first + n_f))
            def _():
                wait_row(row)

    def gw_copy(k):
        return pltpu.make_async_copy(gw_acc.at[k], gw.at[k // 3, lax.rem(k, 3)], gw_sem.at[k])

    for d in range(n_s - 1):
        block = x_peers[d]
        g_wait(block, sibling, h_recv.at[block])
        h_copy(d).wait_send()

        @pl.loop(0, n_f)
        def _(r):
            wide = grads[1, :, lanes(block * n_f + r)].astype(jnp.float32)
            grads[0, :, lanes(block * n_f + r)] = shift_cols(wide, 1).astype(jnp.bfloat16)
            grads[2, :, lanes(block * n_f + r)] = shift_cols(wide, -1).astype(jnp.bfloat16)

        @pl.loop(0, 9)
        def _(k):
            gw_acc[k] += tap(k // 3, lax.rem(k, 3), block)
            if d == n_s - 2:
                gw_copy(k).start()

    gb[...] = lax.dot_general(
        jnp.ones((8, total * cols), jnp.bfloat16), grads[1], NT, preferred_element_type=jnp.float32
    )

    @pl.loop(0, n_f)
    def _(r):
        sum_copy(r).wait_send()

        @pl.when(r == p)
        def _():
            own_out.wait()

        @pl.when(r != p)
        def _():
            out_copy(r).wait_send()
            pltpu.make_async_remote_copy(
                src_ref=act.at[r, :, pl.ds(0, half_c)],
                dst_ref=out.at[0, pl.ds(pl.multiple_of(r * o, o), o), :],
                send_sem=out_send.at[r], recv_sem=out_recv.at[r],
                device_id={"filt": r}, device_id_type=MESH,
            ).wait_recv()

        for d in range(n_s - 1):
            to_x(r, d).wait_send()

        @pl.when((r <= p) & (p + 1 < n_f))
        def _():
            to_right(r).wait_send()

        @pl.when((r >= p) & (p >= 1))
        def _():
            to_left(r).wait_send()

    for d in range(n_s - 1):
        g_copy(d).wait_send()

    @pl.loop(0, 9)
    def _(k):
        gw_copy(k).wait()


def on_device(image, weight, bias, cotangent):
    n_f, n_s, n_in = (lax.axis_size(name) for name in ("filt", "sp", "in"))
    row_count, o, cols = cotangent.shape
    depth = image.shape[2]
    total = n_f * n_s
    any_space = pl.BlockSpec(memory_space=pl.ANY)
    vmem = pl.BlockSpec(memory_space=pltpu.VMEM)
    dma = pltpu.SemaphoreType.DMA
    output, grad_weight, grad_bias = pl.pallas_call(
        functools.partial(kernel, n_f, n_s),
        out_shape=(
            jax.ShapeDtypeStruct((1, n_f * o, cols // n_in), jnp.bfloat16),
            jax.ShapeDtypeStruct((3, 3, o, depth), jnp.float32),
            jax.ShapeDtypeStruct((8, o), jnp.float32),
        ),
        in_specs=[any_space, any_space, vmem, any_space],
        out_specs=(any_space, any_space, vmem),
        scratch_shapes=[
            pltpu.VMEM((total + 2, cols, depth), jnp.bfloat16),
            pltpu.VMEM((3, 3, o, depth), jnp.bfloat16),
            pltpu.VMEM((n_f, o, cols), jnp.bfloat16),
            pltpu.VMEM((n_f, o, cols), jnp.float32),
            pltpu.VMEM((n_f, o, cols), jnp.float32),
            pltpu.VMEM((3, o, total * cols), jnp.bfloat16),
            pltpu.VMEM((n_f, o, cols), jnp.bfloat16),
            pltpu.VMEM((9, o, depth), jnp.float32),
            dma((3,)),
            dma((2, n_f)),
            dma((total,)),
            dma((n_s - 1, n_f)),
            dma((n_f,)),
            dma((n_f,)),
            dma((n_s - 1,)),
            dma((n_s,)),
            dma((n_s - 1,)),
            dma((n_s,)),
            dma((n_f,)),
            dma((n_f,)),
            dma((9,)),
        ],
        compiler_params=pltpu.CompilerParams(
            collective_id=0, has_side_effects=True, vmem_limit_bytes=60 * 1024 * 1024
        ),
    )(image, weight, bias.reshape(1, o), cotangent)
    return (output, grad_weight, grad_bias[0])


def solution(mesh):
    placed = (
        P(("groups", "sp", "filt"), None, "in"),
        P(None, None, "filt", None),
        P("filt"),
        P(("groups", "sp"), "filt", None),
    )
    return jax.shard_map(
        on_device,
        mesh=mesh,
        in_specs=placed,
        out_specs=(
            P(("groups", "sp", "filt"), None, "in"),
            P("groups", None, "filt", "in"),
            P(("groups", "filt")),
        ),
        check_vma=False,
    )
```

time: 230 us -> 60 us (0.26)
  waiting for transfers between devices: 167 us -> 0 us
  Pallas kernels: 0 us -> 51.2 us
  matrix products: 18.4 us -> 0 us
  between operations: 14 us -> 0.64 us
  starting transfers between devices: 9.68 us -> 0 us
  blocking collectives: 5.67 us -> 0 us
  other arithmetic: 5.65 us -> 0 us
    psum x2 -> x0, waiting for transfers between devices: 124 us -> none  [the longest x1 105 us: on_device(): grad_weight, grad_bias = lax.psum((local_weight, local_bias), 'sp')]
    pallas_call x0 -> x1, Pallas kernels: none -> 51.2 us  [on_device(): pl.pallas_call(functools.partial(kernel, n_f, n_s), out_shape=(jax.ShapeD...]
    all_gather x1 -> x0, waiting for transfers between devices: 32.3 us -> none  [on_device(): panel = lax.all_gather(image, 'filt', axis=0, tiled=True)]
    dot_general x18 -> x0, matrix products: 18.4 us -> none  [the longest x9 14.4 us: tap_products(): jnp.einsum('rwc,dc->rdw', window, weight[row_tap, col_tap], preferred_ele...]
    ppermute x2 -> x0, waiting for transfers between devices: 6.09 us -> none  [the longest x1 4.13 us: with_halo(): after = lax.ppermute(initial, axis, down)]
    psum x1 -> x0, blocking collectives: 5.67 us -> none  [on_device(): grad_weight, grad_bias = lax.psum((local_weight, local_bias), 'sp')]
    all_to_all x1 -> x0, starting transfers between devices: 4.88 us -> none  [on_device(): lax.all_to_all(activated.astype(jnp.bfloat16), 'filt', split_axis=0, conc...]
    ppermute x2 -> x0, starting transfers between devices: 4.68 us -> none  [the longest x1 3.39 us: with_halo(): before = lax.ppermute(last, axis, up)]
  transfers between devices with their start and end apart: 6 -> 0, of which waited for: 6 -> 0; matrix products, arithmetic and copies ran while one was open for 1% -> 0% of each run, Pallas kernels for 0% -> 0%
where the time goes in v1:
time: 60 us; the launch traced here: 59.8 us
  Pallas kernels  51.2 us (85%)
  local copies, waits for them, and re-layouts  7.96 us (13%)
  between operations  0.64 us (1%)
    pallas_call x1, Pallas kernels, on_device(): pl.pallas_call(functools.partial(kernel, n_f, n_s), out_shape=(jax.ShapeD...  51.2 us
    unnamed x2, local copies, waits for them, and re-layouts  6.7 us
    slice x1, local copies, waits for them, and re-layouts, on_device(): return (output, grad_weight, grad_bias[0])  1.26 us

profile of v1, /device:TPU:0, one launch (start us, length us, event | category | flops | bytes accessed | tf_op | source)
XLA Modules:
  0.0 59.8 jit_solution(8259609968719332810)
XLA Ops:
  0.6 51.2 %shard_map.67 = (bf16[1,1024,128]{2,1,0:T(8,128)(2,1)}, f32[3,3,256,512]{3,2,1,0:T(8,128)}, f32[8,256]{1,0:T(8,128)}) custom-call(bf16[1,256,512]{2,1,0:T(8,128)(2,1)} %image.1, bf16[3,3,256,1024]{3,2,1,0:T(8,128)(2,1)} %weight.1, f32[1,256]{1,0:T(1,128)} %bitcast.2, bf16[4,256,256]{2,1,0:T(8,128)(2,1)} %cotangent.1), custom_call_target="tpu_custom_call" | custom-call | tf_op jit(solution)/shard_map/pallas_call | solution.py:288
  51.8 1.3 %slice.3 = f32[1,256]{1,0:T(1,128)} slice(f32[8,256]{1,0:T(8,128)} %get-tuple-element.8), slice={[0:1], [0:256]} | slice | bytes 2048 | tf_op jit(solution)/shard_map/slice | solution.py:324
  53.1 1.7 %copy.9 = bf16[1,1024,128]{2,1,0:T(8,128)(2,1)} copy(bf16[1,1024,128]{2,1,0:T(8,128)(2,1)} %get-tuple-element.12) | data formatting | bytes 524288
  54.7 5.0 %copy.10 = f32[3,3,256,512]{3,2,1,0:T(8,128)} copy(f32[3,3,256,512]{3,2,1,0:T(8,128)} %get-tuple-element.13) | data formatting | bytes 9437184

commit v2 on v1

v2 whole, which is shorter than its diff:
```python
import functools

import jax
import jax.numpy as jnp
from jax import lax
from jax.experimental import pallas as pl
from jax.experimental.pallas import tpu as pltpu
from jax.sharding import PartitionSpec as P

MESH = pl.DeviceIdType.MESH
NT = (((1,), (1,)), ((), ()))


def shift_cols(value, by):
    cols = value.shape[1]
    col = lax.broadcasted_iota(jnp.int32, value.shape, 1)
    if by < 0:
        return jnp.where(col == 0, 0.0, pltpu.roll(value, 1, 1))
    return jnp.where(col == cols - 1, 0.0, pltpu.roll(value, cols - 1, 1))


def lanes(q, cols, count=1):
    return pl.ds(pl.multiple_of(q * cols, cols), count * cols)


def store_shifts(grads, place, grad):
    wide = grad.astype(jnp.float32)
    grads[0, :, place] = shift_cols(wide, 1).astype(jnp.bfloat16)
    grads[2, :, place] = shift_cols(wide, -1).astype(jnp.bfloat16)


def block_tap(rows, grads, a, b, block, n_f):
    cols, depth = rows.shape[1], rows.shape[2]
    window = rows[pl.ds(block * n_f + a, n_f)].reshape(n_f * cols, depth)
    return jnp.dot(
        grads[b, :, lanes(block * n_f, cols, n_f)], window, preferred_element_type=jnp.float32
    )


def gather_kernel(
    n_f, n_s,
    image, weight, bias_in, cotangent,
    rows, grads, gw_own, out,
    w, bias, cot, part, peer, act,
    load_sem, row_send, row_recv, x_send, sum_send, sum_recv,
    g_send, g_recv, out_send, out_recv,
):
    p, s, c = lax.axis_index("filt"), lax.axis_index("sp"), lax.axis_index("in")
    sibling = 1 - c
    cols, depth = rows.shape[1], rows.shape[2]
    o = w.shape[2]
    half_c = out.shape[1]
    total = n_f * n_s
    first = s * n_f
    last = n_f - 1
    x_peers = [lax.rem(s + d, n_s) for d in range(1, n_s)]

    load_row = pltpu.make_async_copy(image.at[0], rows.at[1 + first + p], load_sem.at[0])
    load_w = pltpu.make_async_copy(
        weight.at[:, :, :, pl.ds(pl.multiple_of(c * depth, depth), depth)], w, load_sem.at[1]
    )
    load_cot = pltpu.make_async_copy(cotangent, cot, load_sem.at[2])
    load_bias = pltpu.make_async_copy(bias_in, bias, load_sem.at[3])
    load_row.start()
    load_w.start()
    load_cot.start()
    load_bias.start()

    barrier = pltpu.get_barrier_semaphore()
    for d in range(1, n_f):
        pl.semaphore_signal(barrier, 1, device_id={"filt": lax.rem(p + d, n_f)}, device_id_type=MESH)
    for peer_s in x_peers:
        pl.semaphore_signal(barrier, 1, device_id={"sp": peer_s}, device_id_type=MESH)
    pl.semaphore_signal(barrier, 1, device_id={"in": sibling}, device_id_type=MESH)
    pl.semaphore_wait(barrier, n_f - 1 + n_s - 1 + 1)

    def row_copy(q, way, where, send):
        slot = rows.at[1 + q]
        return pltpu.make_async_remote_copy(
            src_ref=slot, dst_ref=slot, send_sem=send, recv_sem=row_recv.at[q],
            device_id={way: where}, device_id_type=MESH,
        )

    def to_right(q):
        return row_copy(q, "filt", p + 1, row_send.at[0, q])

    def to_left(q):
        return row_copy(q, "filt", p - 1, row_send.at[1, q])

    def to_x(q, d):
        return row_copy(first + q, "sp", x_peers[d], x_send.at[d, q])

    def wait_row(q):
        row_copy(q, "filt", p, row_send.at[0, 0]).wait_recv()

    def crosses(q):
        return ((q > 0) & (q < last)) | (q == p)

    def pass_on(q, right, left):
        if right:
            @pl.when(p < last)
            def _():
                to_right(first + q).start()
        if left:
            @pl.when(p > 0)
            def _():
                to_left(first + q).start()

        @pl.when(crosses(q))
        def _():
            for d in range(n_s - 1):
                to_x(q, d).start()

    load_row.wait()
    pass_on(p, True, True)

    zero = jnp.zeros((cols, depth), rows.dtype)
    rows[0] = zero
    rows[total + 1] = zero

    @pl.loop(0, n_f + 2)
    def _(r):
        part[r] = jnp.zeros((o, cols), jnp.float32)

    load_w.wait()

    def add_tap(q, a, r):
        sums = lax.dot_general(
            w[a].reshape(3 * o, depth), rows[1 + q], NT, preferred_element_type=jnp.float32
        )
        part[r + 1] += shift_cols(sums[:o], -1) + sums[o:2 * o] + shift_cols(sums[2 * o:], 1)

    def add_row(q):
        for a in range(3):
            add_tap(first + q, a, q - a + 1)

    def sum_copy(r):
        return pltpu.make_async_remote_copy(
            src_ref=part.at[r + 1], dst_ref=peer.at[r], send_sem=sum_send.at[r], recv_sem=sum_recv.at[r],
            device_id={"in": sibling}, device_id_type=MESH,
        )

    def out_copy(r):
        return pltpu.make_async_remote_copy(
            src_ref=act.at[r, :, pl.ds(pl.multiple_of(c * half_c, half_c), half_c)],
            dst_ref=out.at[pl.ds(pl.multiple_of(p * o, o), o), :],
            send_sem=out_send.at[r], recv_sem=out_recv.at[p],
            device_id={"filt": r}, device_id_type=MESH,
        )

    own_out = pltpu.make_async_copy(
        act.at[p, :, pl.ds(pl.multiple_of(c * half_c, half_c), half_c)],
        out.at[pl.ds(pl.multiple_of(p * o, o), o), :],
        load_sem.at[0],
    )

    def g_copy(q, d):
        place = grads.at[1, :, lanes(q, cols)]
        return pltpu.make_async_remote_copy(
            src_ref=place, dst_ref=place, send_sem=g_send.at[d, q], recv_sem=g_recv.at[q],
            device_id={"sp": x_peers[d]}, device_id_type=MESH,
        )

    def done_at(r):
        low = jnp.where(s == 0, jnp.maximum(p, 1), jnp.maximum(p, n_f - p))
        high = jnp.where(
            s == n_s - 1, jnp.maximum(last - p, 1), jnp.maximum(last - p, p + 1)
        )
        return jnp.where(r == 0, low, jnp.where(r == last, high, jnp.abs(r - p) + 1))

    def finish(r):
        sum_copy(r).wait_recv()
        bias_all = jnp.broadcast_to(bias[...], (cols, o)).T
        shifted = part[r + 1] + peer[r] + bias_all
        sig = jax.nn.sigmoid(shifted)
        slope = sig * (1.0 + shifted * (1.0 - sig))
        grad = (cot[r].astype(jnp.float32) * slope).astype(jnp.bfloat16)
        place = lanes(first + r, cols)
        grads[1, :, place] = grad
        act[r] = (shifted * sig).astype(jnp.bfloat16)
        for d in range(n_s - 1):
            g_copy(first + r, d).start()

        @pl.when(r == p)
        def _():
            own_out.start()

        @pl.when(r != p)
        def _():
            out_copy(r).start()

        store_shifts(grads, place, grad)

    add_row(p)
    load_cot.wait()
    load_bias.wait()

    @pl.loop(1, n_f + 2)
    def _(t):
        @pl.when(p - t >= 0)
        def _():
            wait_row(first + p - t)
            pass_on(p - t, True, False)

        @pl.when(p + t < n_f)
        def _():
            wait_row(first + p + t)
            pass_on(p + t, False, True)

        @pl.when(t == p + 1)
        def _():
            for block in x_peers:
                wait_row(block * n_f)

                @pl.when(p < last)
                def _():
                    to_right(block * n_f).start()

        @pl.when(t == n_f - p)
        def _():
            for block in x_peers:
                wait_row(block * n_f + last)

                @pl.when(p > 0)
                def _():
                    to_left(block * n_f + last).start()

        @pl.when(p - t >= 0)
        def _():
            add_row(p - t)

        @pl.when(p + t < n_f)
        def _():
            add_row(p + t)

        @pl.when((t == p + 1) & (s < n_s - 1))
        def _():
            add_tap(first + n_f, 2, last)

        @pl.when((t == n_f - p) & (s > 0))
        def _():
            add_tap(first - 1, 0, 0)

        @pl.loop(0, n_f)
        def _(r):
            @pl.when(done_at(r) == t)
            def _():
                sum_copy(r).start()

        @pl.loop(0, n_f)
        def _(r):
            @pl.when(done_at(r) == t - 1)
            def _():
                finish(r)

    @pl.loop(0, 9)
    def _(k):
        gw_own[k] = block_tap(rows, grads, k // 3, lax.rem(k, 3), s, n_f)

    for block in x_peers:
        @pl.loop(1, last)
        def _(q):
            wait_row(block * n_f + q)

        @pl.loop(0, n_f)
        def _(q):
            g_copy(block * n_f + q, 0).wait_recv()
            place = lanes(block * n_f + q, cols)
            store_shifts(grads, place, grads[1, :, place])

    @pl.loop(0, n_f)
    def _(r):
        sum_copy(r).wait_send()

        @pl.when(r == p)
        def _():
            own_out.wait()

        @pl.when(r != p)
        def _():
            out_copy(r).wait_send()
            pltpu.make_async_remote_copy(
                src_ref=act.at[r, :, pl.ds(0, half_c)],
                dst_ref=out.at[pl.ds(pl.multiple_of(r * o, o), o), :],
                send_sem=out_send.at[r], recv_sem=out_recv.at[r],
                device_id={"filt": r}, device_id_type=MESH,
            ).wait_recv()

        for d in range(n_s - 1):
            g_copy(first + r, d).wait_send()

            @pl.when(crosses(r))
            def _():
                to_x(r, d).wait_send()

        @pl.when((r <= p) & (p < last))
        def _():
            to_right(first + r).wait_send()

        @pl.when((r >= p) & (p > 0))
        def _():
            to_left(first + r).wait_send()

    for block in x_peers:
        @pl.when(p < last)
        def _():
            to_right(block * n_f).wait_send()

        @pl.when(p > 0)
        def _():
            to_left(block * n_f + last).wait_send()


def finish_kernel(n_f, n_s, rows, grads, gw_own, out_in, gw, gb, out, total, sem, out_sem):
    s = lax.axis_index("sp")
    out_copy = pltpu.make_async_copy(out_in, out.at[0], out_sem)
    out_copy.start()

    def gw_copy(k):
        return pltpu.make_async_copy(total.at[k], gw.at[k // 3, lax.rem(k, 3)], sem.at[k])

    @pl.loop(0, 9)
    def _(k):
        value = gw_own[k]
        for d in range(1, n_s):
            value = value + block_tap(rows, grads, k // 3, lax.rem(k, 3), lax.rem(s + d, n_s), n_f)
        total[k] = value
        gw_copy(k).start()

    gb[...] = lax.dot_general(
        jnp.ones((8, grads.shape[2]), jnp.bfloat16), grads[1], NT, preferred_element_type=jnp.float32
    )[:1]

    @pl.loop(0, 9)
    def _(k):
        gw_copy(k).wait()

    out_copy.wait()


def on_device(image, weight, bias, cotangent):
    n_f, n_s, n_in = (lax.axis_size(name) for name in ("filt", "sp", "in"))
    row_count, o, cols = cotangent.shape
    depth = image.shape[2]
    total = n_f * n_s
    any_space = pl.BlockSpec(memory_space=pl.ANY)
    vmem = pl.BlockSpec(memory_space=pltpu.VMEM)
    hbm = pl.BlockSpec(memory_space=pltpu.HBM)
    dma = pltpu.SemaphoreType.DMA
    between = pl.pallas_call(
        functools.partial(gather_kernel, n_f, n_s),
        out_shape=(
            pltpu.VMEM((total + 2, cols, depth), jnp.bfloat16),
            pltpu.VMEM((3, o, total * cols), jnp.bfloat16),
            pltpu.VMEM((9, o, depth), jnp.float32),
            pltpu.VMEM((n_f * o, cols // n_in), jnp.bfloat16),
        ),
        in_specs=[hbm, hbm, hbm, hbm],
        out_specs=(vmem,) * 4,
        scratch_shapes=[
            pltpu.VMEM((3, 3, o, depth), jnp.bfloat16),
            pltpu.VMEM((1, o), jnp.float32),
            pltpu.VMEM((n_f, o, cols), jnp.bfloat16),
            pltpu.VMEM((n_f + 2, o, cols), jnp.float32),
            pltpu.VMEM((n_f, o, cols), jnp.float32),
            pltpu.VMEM((n_f, o, cols), jnp.bfloat16),
            dma((4,)),
            dma((2, total)),
            dma((total,)),
            dma((n_s - 1, n_f)),
            dma((n_f,)),
            dma((n_f,)),
            dma((n_s - 1, total)),
            dma((total,)),
            dma((n_f,)),
            dma((n_f,)),
        ],
        compiler_params=pltpu.CompilerParams(
            collective_id=0, has_side_effects=True, vmem_limit_bytes=24 * 1024 * 1024
        ),
        name="gather",
    )(*(
        pltpu.with_memory_space_constraint(x, pltpu.HBM)
        for x in (image, weight, bias.reshape(1, o), cotangent)
    ))
    grad_weight, grad_bias, output = pl.pallas_call(
        functools.partial(finish_kernel, n_f, n_s),
        out_shape=(
            jax.ShapeDtypeStruct((3, 3, o, depth), jnp.float32),
            jax.ShapeDtypeStruct((1, o), jnp.float32),
            jax.ShapeDtypeStruct((1, n_f * o, cols // n_in), jnp.bfloat16),
        ),
        in_specs=[vmem] * 4,
        out_specs=(any_space, vmem, any_space),
        scratch_shapes=[
            pltpu.VMEM((9, o, depth), jnp.float32),
            dma((9,)),
            dma(()),
        ],
        compiler_params=pltpu.CompilerParams(vmem_limit_bytes=20 * 1024 * 1024),
        name="finish",
    )(*between)
    return (output, grad_weight, grad_bias.reshape(o))


def solution(mesh):
    placed = (
        P(("groups", "sp", "filt"), None, "in"),
        P(None, None, "filt", None),
        P("filt"),
        P(("groups", "sp"), "filt", None),
    )
    return jax.shard_map(
        on_device,
        mesh=mesh,
        in_specs=placed,
        out_specs=(
            P(("groups", "sp", "filt"), None, "in"),
            P("groups", None, "filt", "in"),
            P(("groups", "filt")),
        ),
        check_vma=False,
    )
```

time: 60 us -> 48.8 us (0.81)
  local copies, waits for them, and re-layouts: 7.96 us -> 0 us
  Pallas kernels: 51.2 us -> 48.1 us
    unnamed x2 -> x0, local copies, waits for them, and re-layouts: 6.7 us -> none
    pallas_call x1 -> x2, Pallas kernels: 51.2 us -> 48.1 us  [the longest x1 42.6 us: on_device(): pl.pallas_call(functools.partial(gather_kernel, n_f, n_s), out_shape=(plt...]
    slice x1 -> x0, local copies, waits for them, and re-layouts: 1.26 us -> none  [on_device(): return (output, grad_weight, grad_bias[0])]
where the time goes in v2:
time: 48.8 us; the launch traced here: 48.7 us
  Pallas kernels  48.1 us (99%)
  between operations  0.64 us (1%)
    pallas_call x1, Pallas kernels, on_device(): pl.pallas_call(functools.partial(gather_kernel, n_f, n_s), out_shape=(plt...  42.6 us
    pallas_call x1, Pallas kernels, on_device(): pl.pallas_call(functools.partial(finish_kernel, n_f, n_s), out_shape=(jax...  5.46 us

profile of v2, /device:TPU:0, one launch (start us, length us, event | category | flops | bytes accessed | tf_op | source)
XLA Modules:
  0.0 48.7 jit_solution(12918953872221586087)
XLA Ops:
  0.6 42.6 %gather.1 = (bf16[10,256,512]{2,1,0:T(8,128)(2,1)S(1)}, bf16[3,256,2048]{2,1,0:T(8,128)(2,1)S(1)}, f32[9,256,512]{2,1,0:T(8,128)S(1)}, bf16[1024,128]{1,0:T(8,128)(2,1)S(1)}) custom-call(bf16[1,256,512]{2,1,0:T(8,128)(2,1)} %image.1, bf16[3,3,256,1024]{3,2,1,0:T(8,128)(2,1)} %weight.1, f32[1,256]{1,0:T(1,128)} %bitcast.2, bf16[4,256,256]{2,1,0:T(8,128)(2,1)} %cotangent.1), custom_call_target="tpu_custom_call" | custom-call | tf_op jit(solution)/shard_map/gather/pallas_call | solution.py:350
  43.2 5.5 %finish.1 = (f32[3,3,256,512]{3,2,1,0:T(8,128)}, f32[1,256]{1,0:T(1,128)}, bf16[1,1024,128]{2,1,0:T(8,128)(2,1)}) custom-call(bf16[10,256,512]{2,1,0:T(8,128)(2,1)S(1)} %get-tuple-element.10.rows, bf16[3,256,2048]{2,1,0:T(8,128)(2,1)S(1)} %get-tuple-element.11.grads, f32[9,256,512]{2,1,0:T(8,128)S(1)} %get-tuple-element.12.gw_own, ...), custom_call_target="tpu_custom_call" | custom-call | tf_op jit(solution)/shard_map/finish/pallas_call | solution.py:386

commit v3 on v2

--- a/solution.py
+++ b/solution.py
@@ -29,12 +29,20 @@
     grads[2, :, place] = shift_cols(wide, -1).astype(jnp.bfloat16)
 
 
-def block_tap(rows, grads, a, b, block, n_f):
+def rows_tap(rows, grads, a, b, start, count):
     cols, depth = rows.shape[1], rows.shape[2]
-    window = rows[pl.ds(block * n_f + a, n_f)].reshape(n_f * cols, depth)
+    window = rows[pl.ds(start + a, count)].reshape(count * cols, depth)
     return jnp.dot(
-        grads[b, :, lanes(block * n_f, cols, n_f)], window, preferred_element_type=jnp.float32
+        grads[b, :, lanes(start, cols, count)], window, preferred_element_type=jnp.float32
     )
+
+
+def late_row(block, n_f):
+    return block * n_f + jnp.where(block > 0, 0, n_f - 1)
+
+
+def early_row(block, n_f):
+    return block * n_f + jnp.where(block > 0, 1, 0)
 
 
 def gather_kernel(
@@ -74,45 +82,48 @@
     pl.semaphore_signal(barrier, 1, device_id={"in": sibling}, device_id_type=MESH)
     pl.semaphore_wait(barrier, n_f - 1 + n_s - 1 + 1)
 
-    def row_copy(q, way, where, send):
-        slot = rows.at[1 + q]
+    piece = cols // 2
+
+    def row_copy(q, h, way, where, send):
+        slot = rows.at[1 + q, pl.ds(h * piece, piece)]
         return pltpu.make_async_remote_copy(
-            src_ref=slot, dst_ref=slot, send_sem=send, recv_sem=row_recv.at[q],
+            src_ref=slot, dst_ref=slot, send_sem=send, recv_sem=row_recv.at[q, h],
             device_id={way: where}, device_id_type=MESH,
         )
 
-    def to_right(q):
-        return row_copy(q, "filt", p + 1, row_send.at[0, q])
-
-    def to_left(q):
-        return row_copy(q, "filt", p - 1, row_send.at[1, q])
-
-    def to_x(q, d):
-        return row_copy(first + q, "sp", x_peers[d], x_send.at[d, q])
-
-    def wait_row(q):
-        row_copy(q, "filt", p, row_send.at[0, 0]).wait_recv()
+    def to_right(q, h):
+        return row_copy(q, h, "filt", p + 1, row_send.at[0, q, h])
+
+    def to_left(q, h):
+        return row_copy(q, h, "filt", p - 1, row_send.at[1, q, h])
+
+    def to_x(q, h, d):
+        return row_copy(first + q, h, "sp", x_peers[d], x_send.at[d, q, h])
+
+    def wait_row(q, h):
+        row_copy(q, h, "filt", p, row_send.at[0, 0, 0]).wait_recv()
 
     def crosses(q):
         return ((q > 0) & (q < last)) | (q == p)
 
-    def pass_on(q, right, left):
+    def pass_on(q, h, right, left):
         if right:
             @pl.when(p < last)
             def _():
-                to_right(first + q).start()
+                to_right(first + q, h).start()
         if left:
             @pl.when(p > 0)
             def _():
-                to_left(first + q).start()
+                to_left(first + q, h).start()
 
         @pl.when(crosses(q))
         def _():
             for d in range(n_s - 1):
-                to_x(q, d).start()
+                to_x(q, h, d).start()
 
     load_row.wait()
-    pass_on(p, True, True)
+    for h in range(2):
+        pass_on(p, h, True, True)
 
     zero = jnp.zeros((cols, depth), rows.dtype)
     rows[0] = zero
@@ -195,44 +206,28 @@
     load_cot.wait()
     load_bias.wait()
 
-    @pl.loop(1, n_f + 2)
-    def _(t):
-        @pl.when(p - t >= 0)
-        def _():
-            wait_row(first + p - t)
-            pass_on(p - t, True, False)
-
-        @pl.when(p + t < n_f)
-        def _():
-            wait_row(first + p + t)
-            pass_on(p + t, False, True)
-
+    def relay(t):
         @pl.when(t == p + 1)
         def _():
             for block in x_peers:
-                wait_row(block * n_f)
-
-                @pl.when(p < last)
-                def _():
-                    to_right(block * n_f).start()
+                for h in range(2):
+                    wait_row(block * n_f, h)
+
+                    @pl.when(p < last)
+                    def _():
+                        to_right(block * n_f, h).start()
 
         @pl.when(t == n_f - p)
         def _():
             for block in x_peers:
-                wait_row(block * n_f + last)
-
-                @pl.when(p > 0)
-                def _():
-                    to_left(block * n_f + last).start()
-
-        @pl.when(p - t >= 0)
-        def _():
-            add_row(p - t)
-
-        @pl.when(p + t < n_f)
-        def _():
-            add_row(p + t)
-
+                for h in range(2):
+                    wait_row(block * n_f + last, h)
+
+                    @pl.when(p > 0)
+                    def _():
+                        to_left(block * n_f + last, h).start()
+
+    def add_edges(t):
         @pl.when((t == p + 1) & (s < n_s - 1))
         def _():
             add_tap(first + n_f, 2, last)
@@ -241,32 +236,85 @@
         def _():
             add_tap(first - 1, 0, 0)
 
+    def start_sums(t):
         @pl.loop(0, n_f)
         def _(r):
             @pl.when(done_at(r) == t)
             def _():
                 sum_copy(r).start()
 
+    def finish_rows(t):
         @pl.loop(0, n_f)
         def _(r):
-            @pl.when(done_at(r) == t - 1)
+            @pl.when(done_at(r) == t)
             def _():
                 finish(r)
 
-    @pl.loop(0, 9)
-    def _(k):
-        gw_own[k] = block_tap(rows, grads, k // 3, lax.rem(k, 3), s, n_f)
+    @pl.loop(1, n_f)
+    def _(t):
+        for h in range(2):
+            @pl.when(p - t >= 0)
+            def _():
+                wait_row(first + p - t, h)
+                pass_on(p - t, h, True, False)
+
+            @pl.when(p + t < n_f)
+            def _():
+                wait_row(first + p + t, h)
+                pass_on(p + t, h, False, True)
+
+        relay(t)
+
+        @pl.when(p - t >= 0)
+        def _():
+            add_row(p - t)
+
+        @pl.when(p + t < n_f)
+        def _():
+            add_row(p + t)
+
+        add_edges(t)
+        start_sums(t)
+        finish_rows(t - 1)
+
+    def own_rows():
+        @pl.loop(0, 9)
+        def _(k):
+            gw_own[k] = rows_tap(rows, grads, k // 3, lax.rem(k, 3), early_row(s, n_f), n_f - 1)
+
+    finish_rows(n_f - 1)
+    if n_s <= 2:
+        own_rows()
+    relay(n_f)
+    add_edges(n_f)
+    start_sums(n_f)
+    finish_rows(n_f)
+    if n_s > 2:
+        own_rows()
+
+    def take_grad(q):
+        g_copy(q, 0).wait_recv()
+        place = lanes(q, cols)
+        store_shifts(grads, place, grads[1, :, place])
 
     for block in x_peers:
+        start = early_row(block, n_f)
+
         @pl.loop(1, last)
         def _(q):
-            wait_row(block * n_f + q)
-
-        @pl.loop(0, n_f)
+            for h in range(2):
+                wait_row(block * n_f + q, h)
+
+        @pl.loop(0, n_f - 1)
         def _(q):
-            g_copy(block * n_f + q, 0).wait_recv()
-            place = lanes(block * n_f + q, cols)
-            store_shifts(grads, place, grads[1, :, place])
+            take_grad(start + q)
+
+        @pl.loop(0, 9)
+        def _(k):
+            gw_own[k] += rows_tap(rows, grads, k // 3, lax.rem(k, 3), start, n_f - 1)
+
+    for block in x_peers:
+        take_grad(late_row(block, n_f))
 
     @pl.loop(0, n_f)
     def _(r):
@@ -291,28 +339,31 @@
 
             @pl.when(crosses(r))
             def _():
-                to_x(r, d).wait_send()
+                for h in range(2):
+                    to_x(r, h, d).wait_send()
 
         @pl.when((r <= p) & (p < last))
         def _():
-            to_right(first + r).wait_send()
+            for h in range(2):
+                to_right(first + r, h).wait_send()
 
         @pl.when((r >= p) & (p > 0))
         def _():
-            to_left(first + r).wait_send()
+            for h in range(2):
+                to_left(first + r, h).wait_send()
 
     for block in x_peers:
-        @pl.when(p < last)
-        def _():
-            to_right(block * n_f).wait_send()
-
-        @pl.when(p > 0)
-        def _():
-            to_left(block * n_f + last).wait_send()
+        for h in range(2):
+            @pl.when(p < last)
+            def _():
+                to_right(block * n_f, h).wait_send()
+
+            @pl.when(p > 0)
+            def _():
+                to_left(block * n_f + last, h).wait_send()
 
 
 def finish_kernel(n_f, n_s, rows, grads, gw_own, out_in, gw, gb, out, total, sem, out_sem):
-    s = lax.axis_index("sp")
     out_copy = pltpu.make_async_copy(out_in, out.at[0], out_sem)
     out_copy.start()
 
@@ -322,8 +373,8 @@
     @pl.loop(0, 9)
     def _(k):
         value = gw_own[k]
-        for d in range(1, n_s):
-            value = value + block_tap(rows, grads, k // 3, lax.rem(k, 3), lax.rem(s + d, n_s), n_f)
+        for block in range(n_s):
+            value = value + rows_tap(rows, grads, k // 3, lax.rem(k, 3), late_row(block, n_f), 1)
         total[k] = value
         gw_copy(k).start()
 
@@ -365,9 +416,9 @@
             pltpu.VMEM((n_f, o, cols), jnp.float32),
             pltpu.VMEM((n_f, o, cols), jnp.bfloat16),
             dma((4,)),
-            dma((2, total)),
-            dma((total,)),
-            dma((n_s - 1, n_f)),
+            dma((2, total, 2)),
+            dma((total, 2)),
+            dma((n_s - 1, n_f, 2)),
             dma((n_f,)),
             dma((n_f,)),
             dma((n_s - 1, total)),

time: 48.8 us -> 46 us (0.943)
  Pallas kernels: 48.1 us -> 45.2 us
    pallas_call x1, Pallas kernels: 42.6 us -> 40.9 us  [on_device(): pl.pallas_call(functools.partial(gather_kernel, n_f, n_s), out_shape=(plt...]
    pallas_call x1, Pallas kernels: 5.46 us -> 4.24 us  [on_device(): pl.pallas_call(functools.partial(finish_kernel, n_f, n_s), out_shape=(jax...]
where the time goes in v3:
time: 46 us; the launch traced here: 45.8 us
  Pallas kernels  45.2 us (98%)
  between operations  0.64 us (1%)
    pallas_call x1, Pallas kernels, on_device(): pl.pallas_call(functools.partial(gather_kernel, n_f, n_s), out_shape=(plt...  40.9 us
    pallas_call x1, Pallas kernels, on_device(): pl.pallas_call(functools.partial(finish_kernel, n_f, n_s), out_shape=(jax...  4.24 us

profile of v3, /device:TPU:0, one launch (start us, length us, event | category | flops | bytes accessed | tf_op | source)
XLA Modules:
  0.0 45.8 jit_solution(12946346064152301272)
XLA Ops:
  0.6 40.9 %gather.1 = (bf16[10,256,512]{2,1,0:T(8,128)(2,1)S(1)}, bf16[3,256,2048]{2,1,0:T(8,128)(2,1)S(1)}, f32[9,256,512]{2,1,0:T(8,128)S(1)}, bf16[1024,128]{1,0:T(8,128)(2,1)S(1)}) custom-call(bf16[1,256,512]{2,1,0:T(8,128)(2,1)} %image.1, bf16[3,3,256,1024]{3,2,1,0:T(8,128)(2,1)} %weight.1, f32[1,256]{1,0:T(1,128)} %bitcast.2, bf16[4,256,256]{2,1,0:T(8,128)(2,1)} %cotangent.1), custom_call_target="tpu_custom_call" | custom-call | tf_op jit(solution)/shard_map/gather/pallas_call | solution.py:401
  41.6 4.2 %finish.1 = (f32[3,3,256,512]{3,2,1,0:T(8,128)}, f32[1,256]{1,0:T(1,128)}, bf16[1,1024,128]{2,1,0:T(8,128)(2,1)}) custom-call(bf16[10,256,512]{2,1,0:T(8,128)(2,1)S(1)} %get-tuple-element.10.rows, bf16[3,256,2048]{2,1,0:T(8,128)(2,1)S(1)} %get-tuple-element.11.grads, f32[9,256,512]{2,1,0:T(8,128)S(1)} %get-tuple-element.12.gw_own, ...), custom_call_target="tpu_custom_call" | custom-call | tf_op jit(solution)/shard_map/finish/pallas_call | solution.py:437

commit v4 on v3

--- a/solution.py
+++ b/solution.py
@@ -192,6 +192,9 @@
         for d in range(n_s - 1):
             g_copy(first + r, d).start()
 
+        store_shifts(grads, place, grad)
+
+    def send_out(r):
         @pl.when(r == p)
         def _():
             own_out.start()
@@ -199,8 +202,6 @@
         @pl.when(r != p)
         def _():
             out_copy(r).start()
-
-        store_shifts(grads, place, grad)
 
     add_row(p)
     load_cot.wait()
@@ -288,7 +289,21 @@
     relay(n_f)
     add_edges(n_f)
     start_sums(n_f)
+
+    @pl.loop(0, n_f)
+    def _(r):
+        @pl.when(done_at(r) < n_f)
+        def _():
+            send_out(r)
+
     finish_rows(n_f)
+
+    @pl.loop(0, n_f)
+    def _(r):
+        @pl.when(done_at(r) == n_f)
+        def _():
+            send_out(r)
+
     if n_s > 2:
         own_rows()
 
@@ -367,14 +382,16 @@
     out_copy = pltpu.make_async_copy(out_in, out.at[0], out_sem)
     out_copy.start()
 
+    late = [(n_f - 1, min(n_s, 2))] + [(block * n_f, 1) for block in range(2, n_s)]
+
     def gw_copy(k):
         return pltpu.make_async_copy(total.at[k], gw.at[k // 3, lax.rem(k, 3)], sem.at[k])
 
     @pl.loop(0, 9)
     def _(k):
         value = gw_own[k]
-        for block in range(n_s):
-            value = value + rows_tap(rows, grads, k // 3, lax.rem(k, 3), late_row(block, n_f), 1)
+        for start, count in late:
+            value = value + rows_tap(rows, grads, k // 3, lax.rem(k, 3), start, count)
         total[k] = value
         gw_copy(k).start()
 

time: 46 us -> 45.9 us (level)
  no operation moved by 1% of the time
where the time goes in v4:
time: 45.9 us; the launch traced here: 45.7 us
  Pallas kernels  45.1 us (98%)
  between operations  0.64 us (1%)
    pallas_call x1, Pallas kernels, on_device(): pl.pallas_call(functools.partial(gather_kernel, n_f, n_s), out_shape=(plt...  40.8 us
    pallas_call x1, Pallas kernels, on_device(): pl.pallas_call(functools.partial(finish_kernel, n_f, n_s), out_shape=(jax...  4.24 us

profile of v4, /device:TPU:0, one launch (start us, length us, event | category | flops | bytes accessed | tf_op | source)
XLA Modules:
  0.0 45.7 jit_solution(14558234658147046237)
XLA Ops:
  0.6 40.8 %gather.1 = (bf16[10,256,512]{2,1,0:T(8,128)(2,1)S(1)}, bf16[3,256,2048]{2,1,0:T(8,128)(2,1)S(1)}, f32[9,256,512]{2,1,0:T(8,128)S(1)}, bf16[1024,128]{1,0:T(8,128)(2,1)S(1)}) custom-call(bf16[1,256,512]{2,1,0:T(8,128)(2,1)} %image.1, bf16[3,3,256,1024]{3,2,1,0:T(8,128)(2,1)} %weight.1, f32[1,256]{1,0:T(1,128)} %bitcast.2, bf16[4,256,256]{2,1,0:T(8,128)(2,1)} %cotangent.1), custom_call_target="tpu_custom_call" | custom-call | tf_op jit(solution)/shard_map/gather/pallas_call | solution.py:418
  41.5 4.2 %finish.1 = (f32[3,3,256,512]{3,2,1,0:T(8,128)}, f32[1,256]{1,0:T(1,128)}, bf16[1,1024,128]{2,1,0:T(8,128)(2,1)}) custom-call(bf16[10,256,512]{2,1,0:T(8,128)(2,1)S(1)} %get-tuple-element.10.rows, bf16[3,256,2048]{2,1,0:T(8,128)(2,1)S(1)} %get-tuple-element.11.grads, f32[9,256,512]{2,1,0:T(8,128)S(1)} %get-tuple-element.12.gw_own, ...), custom_call_target="tpu_custom_call" | custom-call | tf_op jit(solution)/shard_map/finish/pallas_call | solution.py:454

commit v5 on v4

--- a/solution.py
+++ b/solution.py
@@ -51,7 +51,7 @@
     rows, grads, gw_own, out,
     w, bias, cot, part, peer, act,
     load_sem, row_send, row_recv, x_send, sum_send, sum_recv,
-    g_send, g_recv, out_send, out_recv,
+    g_send, g_recv, h_send, h_recv, out_send, out_recv,
 ):
     p, s, c = lax.axis_index("filt"), lax.axis_index("sp"), lax.axis_index("in")
     sibling = 1 - c
@@ -165,11 +165,23 @@
         load_sem.at[0],
     )
 
+    half_o = o // 2
+
+    def g_half(q, core):
+        return grads.at[1, pl.ds(pl.multiple_of(core * half_o, half_o), half_o), lanes(q, cols)]
+
     def g_copy(q, d):
-        place = grads.at[1, :, lanes(q, cols)]
+        place = g_half(q, c)
         return pltpu.make_async_remote_copy(
             src_ref=place, dst_ref=place, send_sem=g_send.at[d, q], recv_sem=g_recv.at[q],
             device_id={"sp": x_peers[d]}, device_id_type=MESH,
+        )
+
+    def h_copy(q, core):
+        place = g_half(q, core)
+        return pltpu.make_async_remote_copy(
+            src_ref=place, dst_ref=place, send_sem=h_send.at[q], recv_sem=h_recv.at[q],
+            device_id={"in": sibling}, device_id_type=MESH,
         )
 
     def done_at(r):
@@ -307,8 +319,12 @@
     if n_s > 2:
         own_rows()
 
+    def share_grad(q):
+        g_copy(q, 0).wait_recv()
+        h_copy(q, c).start()
+
     def take_grad(q):
-        g_copy(q, 0).wait_recv()
+        h_copy(q, sibling).wait_recv()
         place = lanes(q, cols)
         store_shifts(grads, place, grads[1, :, place])
 
@@ -322,6 +338,10 @@
 
         @pl.loop(0, n_f - 1)
         def _(q):
+            share_grad(start + q)
+
+        @pl.loop(0, n_f - 1)
+        def _(q):
             take_grad(start + q)
 
         @pl.loop(0, 9)
@@ -329,6 +349,7 @@
             gw_own[k] += rows_tap(rows, grads, k // 3, lax.rem(k, 3), start, n_f - 1)
 
     for block in x_peers:
+        share_grad(late_row(block, n_f))
         take_grad(late_row(block, n_f))
 
     @pl.loop(0, n_f)
@@ -368,6 +389,10 @@
                 to_left(first + r, h).wait_send()
 
     for block in x_peers:
+        @pl.loop(0, n_f)
+        def _(q):
+            h_copy(block * n_f + q, c).wait_send()
+
         for h in range(2):
             @pl.when(p < last)
             def _():
@@ -440,6 +465,8 @@
             dma((n_f,)),
             dma((n_s - 1, total)),
             dma((total,)),
+            dma((total,)),
+            dma((total,)),
             dma((n_f,)),
             dma((n_f,)),
         ],

time: 45.9 us -> 43.8 us (0.954)
  Pallas kernels: 45.1 us -> 43 us
    pallas_call x1, Pallas kernels: 40.8 us -> 38.8 us  [on_device(): pl.pallas_call(functools.partial(gather_kernel, n_f, n_s), out_shape=(plt...]
where the time goes in v5:
time: 43.8 us; the launch traced here: 43.7 us
  Pallas kernels  43 us (98%)
  between operations  0.64 us (1%)
    pallas_call x1, Pallas kernels, on_device(): pl.pallas_call(functools.partial(gather_kernel, n_f, n_s), out_shape=(plt...  38.8 us
    pallas_call x1, Pallas kernels, on_device(): pl.pallas_call(functools.partial(finish_kernel, n_f, n_s), out_shape=(jax...  4.24 us

profile of v5, /device:TPU:0, one launch (start us, length us, event | category | flops | bytes accessed | tf_op | source)
XLA Modules:
  0.0 43.7 jit_solution(11111342838921641314)
XLA Ops:
  0.6 38.8 %gather.1 = (bf16[10,256,512]{2,1,0:T(8,128)(2,1)S(1)}, bf16[3,256,2048]{2,1,0:T(8,128)(2,1)S(1)}, f32[9,256,512]{2,1,0:T(8,128)S(1)}, bf16[1024,128]{1,0:T(8,128)(2,1)S(1)}) custom-call(bf16[1,256,512]{2,1,0:T(8,128)(2,1)} %image.1, bf16[3,3,256,1024]{3,2,1,0:T(8,128)(2,1)} %weight.1, f32[1,256]{1,0:T(1,128)} %bitcast.2, bf16[4,256,256]{2,1,0:T(8,128)(2,1)} %cotangent.1), custom_call_target="tpu_custom_call" | custom-call | tf_op jit(solution)/shard_map/gather/pallas_call | solution.py:443
  39.4 4.2 %finish.1 = (f32[3,3,256,512]{3,2,1,0:T(8,128)}, f32[1,256]{1,0:T(1,128)}, bf16[1,1024,128]{2,1,0:T(8,128)(2,1)}) custom-call(bf16[10,256,512]{2,1,0:T(8,128)(2,1)S(1)} %get-tuple-element.10.rows, bf16[3,256,2048]{2,1,0:T(8,128)(2,1)S(1)} %get-tuple-element.11.grads, f32[9,256,512]{2,1,0:T(8,128)S(1)} %get-tuple-element.12.gw_own, ...), custom_call_target="tpu_custom_call" | custom-call | tf_op jit(solution)/shard_map/finish/pallas_call | solution.py:481

commit v6 on v5

--- a/solution.py
+++ b/solution.py
@@ -103,8 +103,8 @@
     def wait_row(q, h):
         row_copy(q, h, "filt", p, row_send.at[0, 0, 0]).wait_recv()
 
-    def crosses(q):
-        return ((q > 0) & (q < last)) | (q == p)
+    def crosses(q, h):
+        return ((q > 0) & (q < last)) | (q == p) | (h == 1)
 
     def pass_on(q, h, right, left):
         if right:
@@ -116,7 +116,7 @@
             def _():
                 to_left(first + q, h).start()
 
-        @pl.when(crosses(q))
+        @pl.when(crosses(q, h))
         def _():
             for d in range(n_s - 1):
                 to_x(q, h, d).start()
@@ -223,22 +223,24 @@
         @pl.when(t == p + 1)
         def _():
             for block in x_peers:
-                for h in range(2):
-                    wait_row(block * n_f, h)
-
-                    @pl.when(p < last)
-                    def _():
-                        to_right(block * n_f, h).start()
+                wait_row(block * n_f, 0)
+
+                @pl.when(p < last)
+                def _():
+                    to_right(block * n_f, 0).start()
+
+                wait_row(block * n_f, 1)
 
         @pl.when(t == n_f - p)
         def _():
             for block in x_peers:
-                for h in range(2):
-                    wait_row(block * n_f + last, h)
-
-                    @pl.when(p > 0)
-                    def _():
-                        to_left(block * n_f + last, h).start()
+                wait_row(block * n_f + last, 0)
+
+                @pl.when(p > 0)
+                def _():
+                    to_left(block * n_f + last, 0).start()
+
+                wait_row(block * n_f + last, 1)
 
     def add_edges(t):
         @pl.when((t == p + 1) & (s < n_s - 1))
@@ -373,9 +375,9 @@
         for d in range(n_s - 1):
             g_copy(first + r, d).wait_send()
 
-            @pl.when(crosses(r))
-            def _():
-                for h in range(2):
+            for h in range(2):
+                @pl.when(crosses(r, h))
+                def _():
                     to_x(r, h, d).wait_send()
 
         @pl.when((r <= p) & (p < last))
@@ -393,14 +395,13 @@
         def _(q):
             h_copy(block * n_f + q, c).wait_send()
 
-        for h in range(2):
-            @pl.when(p < last)
-            def _():
-                to_right(block * n_f, h).wait_send()
-
-            @pl.when(p > 0)
-            def _():
-                to_left(block * n_f + last, h).wait_send()
+        @pl.when(p < last)
+        def _():
+            to_right(block * n_f, 0).wait_send()
+
+        @pl.when(p > 0)
+        def _():
+            to_left(block * n_f + last, 0).wait_send()
 
 
 def finish_kernel(n_f, n_s, rows, grads, gw_own, out_in, gw, gb, out, total, sem, out_sem):

time: 43.8 us -> 44.1 us (level)
  no operation moved by 1% of the time
where the time goes in v6:
time: 44.1 us; the launch traced here: 43.9 us
  Pallas kernels  43.3 us (98%)
  between operations  0.64 us (1%)
    pallas_call x1, Pallas kernels, on_device(): pl.pallas_call(functools.partial(gather_kernel, n_f, n_s), out_shape=(plt...  39.1 us
    pallas_call x1, Pallas kernels, on_device(): pl.pallas_call(functools.partial(finish_kernel, n_f, n_s), out_shape=(jax...  4.24 us

profile of v6, /device:TPU:0, one launch (start us, length us, event | category | flops | bytes accessed | tf_op | source)
XLA Modules:
  0.0 43.9 jit_solution(17745202285317900212)
XLA Ops:
  0.6 39.1 %gather.1 = (bf16[10,256,512]{2,1,0:T(8,128)(2,1)S(1)}, bf16[3,256,2048]{2,1,0:T(8,128)(2,1)S(1)}, f32[9,256,512]{2,1,0:T(8,128)S(1)}, bf16[1024,128]{1,0:T(8,128)(2,1)S(1)}) custom-call(bf16[1,256,512]{2,1,0:T(8,128)(2,1)} %image.1, bf16[3,3,256,1024]{3,2,1,0:T(8,128)(2,1)} %weight.1, f32[1,256]{1,0:T(1,128)} %bitcast.2, bf16[4,256,256]{2,1,0:T(8,128)(2,1)} %cotangent.1), custom_call_target="tpu_custom_call" | custom-call | tf_op jit(solution)/shard_map/gather/pallas_call | solution.py:444
  39.7 4.2 %finish.1 = (f32[3,3,256,512]{3,2,1,0:T(8,128)}, f32[1,256]{1,0:T(1,128)}, bf16[1,1024,128]{2,1,0:T(8,128)(2,1)}) custom-call(bf16[10,256,512]{2,1,0:T(8,128)(2,1)S(1)} %get-tuple-element.10.rows, bf16[3,256,2048]{2,1,0:T(8,128)(2,1)S(1)} %get-tuple-element.11.grads, f32[9,256,512]{2,1,0:T(8,128)S(1)} %get-tuple-element.12.gw_own, ...), custom_call_target="tpu_custom_call" | custom-call | tf_op jit(solution)/shard_map/finish/pallas_call | solution.py:482
